TPU v7x, 32 devices: a whole 2x2x4 slice. The times are simulated.
32 devices in a mesh: groups: 2 (over x), patch: 16 (over z, y, core).
Axes of the slice: x: 2, y: 2, z: 4, core: 2. Of those that a mesh axis runs over, the one named last changes fastest.
Arguments:
- points: bfloat16 [32768, 512], P(('groups', 'patch')), parts along dimension 0, may hold values from -6 to 6
- lengths: int32 [32], P(('groups', 'patch')), parts along dimension 0, may hold values from 1 to 1024, 12288 in all
- send_blocks: int32 [32, 2, 3], P(('groups', 'patch')), parts along dimension 0, may hold values from 0 to 7, as said below
- pattern: int32 [256, 3], P(('groups', 'patch')), parts along dimension 0, may hold values from 0 to 13, as said below
- ln1_gain: float32 [512], replicated, may hold values from 0.25 to 1.75
- qk_weight: bfloat16 [2, 512, 512], replicated
- v_weight: bfloat16 [512, 512], replicated, may hold values from -0.25 to 0.25
- o_weight: bfloat16 [512, 512], replicated, may hold values from -0.25 to 0.25
- ln2_gain: float32 [512], replicated, may hold values from 0.25 to 1.75
- up_weight: bfloat16 [512, 2048], replicated, may hold values from -0.25 to 0.25
- down_weight: bfloat16 [2048, 512], replicated, may hold values from -0.125 to 0.125
Outputs:
- block_out: bfloat16 [32768, 512], P(('groups', 'patch')), parts along dimension 0
There are 2 independent parts, one for each index of `groups`. A program takes and returns all parts, laid end to end along the dimension named above; an argument that names none is the same for every part. Nothing has to cross between parts.
Inputs may be any that keep to these rules, and one draw needn't show every extreme that they name: `send_blocks`: for each patch the 6 entries are distinct local blocks; [p, 0, :] are offered to patch p - 1 and [p, 1, :] to patch p + 1. `pattern`: row r belongs to block r % 8 of patch r // 8; its entries are distinct slots other than r % 8; the first patch names no slot from 8 to 10, the last patch no slot from 11 on. `lengths`: they sum to 12288; some patch is full.
All inputs are finite; a program needn't handle non-finite values. No bound on the sum of `lengths` on one device may be relied on, other than what follows from the above.
Results may differ from a plain program's by a relative error of at most 0.011.
Values may be sent and summed in bfloat16 or wider, within the bound.
A program may use at most 64 MiB of HBM per device.

v0:
```python
import math

import jax
import jax.numpy as jnp
from jax import lax
from jax.sharding import PartitionSpec as P

H = 32


def passed_along(array, axis, by):
    count = lax.axis_size(axis)
    pairs = [(i, i + by) for i in range(count) if 0 <= i + by < count]
    return lax.ppermute(array, axis, pairs)


def layer_norm(inputs, gain):
    center = inputs - jnp.mean(inputs, axis=-1, keepdims=True)
    spread = jnp.mean(center * center, axis=-1, keepdims=True)
    return center * lax.rsqrt(spread + 1e-05) * gain


def project_blocks(blocks, weight):
    shape = blocks.shape
    flat = jnp.dot(blocks.reshape(-1, shape[-1]), weight, preferred_element_type=jnp.float32)
    return flat.astype(jnp.bfloat16).reshape(shape[:-1] + (weight.shape[1],))


def attend_blocks(queries, pool_keys, pool_values, pool_bias, picks, heads, head_size):
    scale = 1.0 / math.sqrt(head_size)

    def one_block(index):
        chosen = jnp.concatenate([index[None], picks[index]])
        key_rows = jnp.take(pool_keys, chosen, axis=0).reshape(-1, heads, head_size)
        value_rows = jnp.take(pool_values, chosen, axis=0).reshape(-1, heads, head_size)
        bias_rows = jnp.take(pool_bias, chosen, axis=0).reshape(-1).astype(jnp.float32)
        scores = (
            jnp.einsum("qhd,khd->hqk", queries[index], key_rows, preferred_element_type=jnp.float32)
            * scale
        )
        scores = scores + bias_rows[None, None, :]
        top = jnp.max(scores, axis=-1, keepdims=True)
        expo = jnp.exp(scores - top)
        weights = (expo / jnp.sum(expo, axis=-1, keepdims=True)).astype(jnp.bfloat16)
        mixed = jnp.einsum("hqk,khd->qhd", weights, value_rows, preferred_element_type=jnp.float32)
        return mixed.astype(jnp.bfloat16)

    return lax.map(one_block, jnp.arange(queries.shape[0], dtype=jnp.int32))


def on_device(
    points,
    lengths,
    send_blocks,
    pattern,
    ln1_gain,
    qk_weight,
    v_weight,
    o_weight,
    ln2_gain,
    up_weight,
    down_weight,
):
    row_count = points.shape[0]
    width = points.shape[1]
    block_count = pattern.shape[0]
    block_rows = row_count // block_count
    heads = H
    head_size = width // heads
    inputs = points.astype(jnp.float32)
    normed = layer_norm(inputs, ln1_gain).astype(jnp.bfloat16)
    queries = jnp.dot(normed, qk_weight[0], preferred_element_type=jnp.float32).astype(jnp.bfloat16)
    keys_local = jnp.dot(normed, qk_weight[1], preferred_element_type=jnp.float32).astype(
        jnp.bfloat16
    )
    values_local = jnp.dot(normed, v_weight, preferred_element_type=jnp.float32).astype(
        jnp.bfloat16
    )
    valid = jnp.arange(row_count, dtype=jnp.int32) < lengths[0]
    key_bias = jnp.where(valid, 0.0, -1000000000.0).astype(jnp.bfloat16)
    key_blocks = keys_local.reshape(block_count, block_rows, width)
    value_blocks = values_local.reshape(block_count, block_rows, width)
    bias_blocks = key_bias.reshape(block_count, block_rows)
    to_right = send_blocks[0, 1]
    to_left = send_blocks[0, 0]
    normed_blocks = normed.reshape(block_count, block_rows, width)
    left_rows, left_bias = passed_along(
        (normed_blocks[to_right], bias_blocks[to_right]), "patch", 1
    )
    right_rows, right_bias = passed_along(
        (normed_blocks[to_left], bias_blocks[to_left]), "patch", -1
    )
    left_keys = project_blocks(left_rows, qk_weight[1])
    left_values = project_blocks(left_rows, v_weight)
    right_keys = project_blocks(right_rows, qk_weight[1])
    right_values = project_blocks(right_rows, v_weight)
    pool_keys = jnp.concatenate([key_blocks, left_keys, right_keys], axis=0)
    pool_values = jnp.concatenate([value_blocks, left_values, right_values], axis=0)
    pool_bias = jnp.concatenate([bias_blocks, left_bias, right_bias], axis=0)
    query_blocks = queries.reshape(block_count, block_rows, heads, head_size)
    attended = attend_blocks(
        query_blocks, pool_keys, pool_values, pool_bias, pattern, heads, head_size
    ).reshape(row_count, width)
    mixed = inputs + jnp.dot(attended, o_weight, preferred_element_type=jnp.float32)
    normed_two = layer_norm(mixed, ln2_gain).astype(jnp.bfloat16)
    hidden = jax.nn.gelu(
        jnp.dot(normed_two, up_weight, preferred_element_type=jnp.float32), approximate=False
    ).astype(jnp.bfloat16)
    result = mixed + jnp.dot(hidden, down_weight, preferred_element_type=jnp.float32)
    return jnp.where(valid[:, None], result, 0.0).astype(jnp.bfloat16)


def solution(mesh):
    in_specs = (
        P(("groups", "patch"), None),
        P(("groups", "patch")),
        P(("groups", "patch"), None, None),
        P(("groups", "patch"), None),
        P(),
        P(),
        P(),
        P(),
        P(),
        P(),
        P(),
    )
    out_specs = P(("groups", "patch"), None)
    return jax.shard_map(
        on_device, mesh=mesh, in_specs=in_specs, out_specs=out_specs, check_vma=False
    )
```

profile of v0, /device:TPU:25, one launch (start us, length us, event | category | flops | bytes accessed | tf_op | source)
XLA Modules:
  0.0 292.8 jit_solution(8000591927344690779)
XLA Ops:
  9.0 3.7 %collective-permute-start = (bf16[3,128,512]{2,1,0:T(8,128)(2,1)}, bf16[3,128,512]{2,1,0:T(8,128)(2,1)S(1)}, u32[]{:S(2)}, u32[]{:S(2)}) collective-permute-start(bf16[3,128,512]{2,1,0:T(8,128)(2,1)} %gather_fusion.3), channel_id=1, source_target_pairs={{0,1},{1,2},{2,3},{3,4},{4,5},{5,6},{6,7},{7,8},{8,9},{9,10},{10,1... | collective-permute-start | bytes 1179656 | tf_op jit(solution)/shard_map/ppermute | solution.py:14
  19.1 3.6 %collective-permute-start.2 = (bf16[3,128]{1,0:T(4,128)(2,1)}, bf16[3,128]{1,0:T(4,128)(2,1)}, u32[]{:S(2)}, u32[]{:S(2)}) collective-permute-start(bf16[3,128]{1,0:T(4,128)(2,1)} %gather_fusion.5), channel_id=1, source_target_pairs={{0,1},{1,2},{2,3},{3,4},{4,5},{5,6},{6,7},{7,8},{8,9},{9,10},{10,1... | collective-permute-start | bytes 2312 | tf_op jit(solution)/shard_map/ppermute | solution.py:14
  25.2 3.1 %convolution_convert_fusion = bf16[1024,512]{1,0:T(8,128)(2,1)} fusion(bf16[1024,512]{0,1:T(8,128)(2,1)} %fusion.47, bf16[2,512,512]{2,1,0:T(8,128)(2,1)} %param.20), kind=kOutput, calls=%fused_computation.73 | convolution fusion | flops 537395200 | bytes 2621440 | tf_op jit(solution)/shard_map/dot_general | solution.py:73
  28.3 3.1 %convolution_convert_fusion.1 = bf16[1024,512]{1,0:T(8,128)(2,1)} fusion(bf16[1024,512]{0,1:T(8,128)(2,1)} %fusion.47, bf16[2,512,512]{2,1,0:T(8,128)(2,1)} %param.20), kind=kOutput, calls=%fused_computation.74 | convolution fusion | flops 537395200 | bytes 2621440 | tf_op jit(solution)/shard_map/dot_general | solution.py:72
  31.4 3.1 %convolution_convert_fusion.2 = bf16[1024,512]{1,0:T(8,128)(2,1)} fusion(bf16[1024,512]{0,1:T(8,128)(2,1)} %fusion.47, bf16[512,512]{1,0:T(8,128)(2,1)} %param.21), kind=kOutput, calls=%fused_computation.75 | convolution fusion | flops 537395200 | bytes 2621440 | tf_op jit(solution)/shard_map/dot_general | solution.py:76
  44.8 3.3 %pad_maximum_fusion = (bf16[14,128,512]{2,1,0:T(8,128)(2,1)}, bf16[14,128,512]{2,1,0:T(8,128)(2,1)}) fusion(bf16[3,128,512]{2,1,0:T(8,128)(2,1)S(1)} %bitcast.118, bf16[3,128,512]{2,1,0:T(8,128)(2,1)S(1)} %bitcast.117, bf16[8,128,512]{2,1,0:T(8,128)(2,1)} %bitcast.120, bf16[3,128,512]{2,1,0:T(8,128)(2,1)S(1)} %bitcast.122, ...), kind=kLoop, calls=%fused_computation.71 | loop fusion | flops 3670016 | bytes 7340032 | tf_op jit(solution)/shard_map/concatenate | solution.py:98
  48.1 212.9 %while.10 = (s32[]{:T(128)}, bf16[8,128,32,16]{1,3,2,0:T(8,128)(2,1)}, s32[8]{0:T(128)S(1)}, s32[8,3]{1,0:T(8,128)S(1)}, bf16[14,128,512]{2,1,0:T(8,128)(2,1)}, ...) while((s32[]{:T(128)}, ...), condition=%wide.region_5.7_spmd, body=%wide.region_2.6_spmd.sunk | while | flops 147394096 | bytes 26525540 | solution.py:48
  54.2 2.9 gather_fusion.1
  62.0 6.8 %fusion.132 = (f32[32,128]{1,0:T(8,128)S(1)}, f32[32,128,512]{2,1,0:T(8,128)}) fusion(f32[512]{0:T(512)S(1)} %bitcast_convert_fusion.2, bf16[512,32,16]{0,2,1:T(8,128)(2,1)S(1)} %reshape.337, bf16[8,128,32,16]{1,3,2,0:T(8,128)(2,1)} %get-tuple-element.187, s32[]{:T(128)S(6)} %select_n.100), kind=kOutput, calls=%fused_computation.137.clone.1 | convolution fusion | flops 75497984 | bytes 9062404 | tf_op jit(solution)/shard_map/while/body/eval_jaxpr/sub | solution.py:43
  69.3 5.3 %fusion.133 = bf16[8,128,32,16]{1,3,2,0:T(8,128)(2,1)} fusion(bf16[8,128,32,16]{1,3,2,0:T(8,128)(2,1)} %get-tuple-element.172, s32[]{:T(128)} %get-tuple-element.171, bf16[512,32,16]{0,2,1:T(8,128)(2,1)S(1)} %reshape.336, f32[32,128,512]{2,1,0:T(8,128)} %get-tuple-element.158, f32[32,128]{1,0:T(8,128)S(1)} %get-tuple-element.159), kind=kOutput, calls=%fused_computation.18.clone.1 | convolution fusion | flops 71368704 | bytes 9060864 | tf_op jit(solution)/shard_map/while/body/eval_jaxpr/hqk,khd->qhd/dot_general | solution.py:45
  80.8 2.9 gather_fusion.1
  88.6 6.8 %fusion.132 = (f32[32,128]{1,0:T(8,128)S(1)}, f32[32,128,512]{2,1,0:T(8,128)}) fusion(f32[512]{0:T(512)S(1)} %bitcast_convert_fusion.2, bf16[512,32,16]{0,2,1:T(8,128)(2,1)S(1)} %reshape.337, bf16[8,128,32,16]{1,3,2,0:T(8,128)(2,1)} %get-tuple-element.187, s32[]{:T(128)S(6)} %select_n.100), kind=kOutput, calls=%fused_computation.137.clone.1 | convolution fusion | flops 75497984 | bytes 9062404 | tf_op jit(solution)/shard_map/while/body/eval_jaxpr/sub | solution.py:43
  95.9 5.3 %fusion.133 = bf16[8,128,32,16]{1,3,2,0:T(8,128)(2,1)} fusion(bf16[8,128,32,16]{1,3,2,0:T(8,128)(2,1)} %get-tuple-element.172, s32[]{:T(128)} %get-tuple-element.171, bf16[512,32,16]{0,2,1:T(8,128)(2,1)S(1)} %reshape.336, f32[32,128,512]{2,1,0:T(8,128)} %get-tuple-element.158, f32[32,128]{1,0:T(8,128)S(1)} %get-tuple-element.159), kind=kOutput, calls=%fused_computation.18.clone.1 | convolution fusion | flops 71368704 | bytes 9060864 | tf_op jit(solution)/shard_map/while/body/eval_jaxpr/hqk,khd->qhd/dot_general | solution.py:45
  107.4 2.9 gather_fusion.1
  115.3 6.8 %fusion.132 = (f32[32,128]{1,0:T(8,128)S(1)}, f32[32,128,512]{2,1,0:T(8,128)}) fusion(f32[512]{0:T(512)S(1)} %bitcast_convert_fusion.2, bf16[512,32,16]{0,2,1:T(8,128)(2,1)S(1)} %reshape.337, bf16[8,128,32,16]{1,3,2,0:T(8,128)(2,1)} %get-tuple-element.187, s32[]{:T(128)S(6)} %select_n.100), kind=kOutput, calls=%fused_computation.137.clone.1 | convolution fusion | flops 75497984 | bytes 9062404 | tf_op jit(solution)/shard_map/while/body/eval_jaxpr/sub | solution.py:43
  122.5 5.3 %fusion.133 = bf16[8,128,32,16]{1,3,2,0:T(8,128)(2,1)} fusion(bf16[8,128,32,16]{1,3,2,0:T(8,128)(2,1)} %get-tuple-element.172, s32[]{:T(128)} %get-tuple-element.171, bf16[512,32,16]{0,2,1:T(8,128)(2,1)S(1)} %reshape.336, f32[32,128,512]{2,1,0:T(8,128)} %get-tuple-element.158, f32[32,128]{1,0:T(8,128)S(1)} %get-tuple-element.159), kind=kOutput, calls=%fused_computation.18.clone.1 | convolution fusion | flops 71368704 | bytes 9060864 | tf_op jit(solution)/shard_map/while/body/eval_jaxpr/hqk,khd->qhd/dot_general | solution.py:45
  134.0 2.9 gather_fusion.1
  141.9 6.8 %fusion.132 = (f32[32,128]{1,0:T(8,128)S(1)}, f32[32,128,512]{2,1,0:T(8,128)}) fusion(f32[512]{0:T(512)S(1)} %bitcast_convert_fusion.2, bf16[512,32,16]{0,2,1:T(8,128)(2,1)S(1)} %reshape.337, bf16[8,128,32,16]{1,3,2,0:T(8,128)(2,1)} %get-tuple-element.187, s32[]{:T(128)S(6)} %select_n.100), kind=kOutput, calls=%fused_computation.137.clone.1 | convolution fusion | flops 75497984 | bytes 9062404 | tf_op jit(solution)/shard_map/while/body/eval_jaxpr/sub | solution.py:43
  149.2 5.3 %fusion.133 = bf16[8,128,32,16]{1,3,2,0:T(8,128)(2,1)} fusion(bf16[8,128,32,16]{1,3,2,0:T(8,128)(2,1)} %get-tuple-element.172, s32[]{:T(128)} %get-tuple-element.171, bf16[512,32,16]{0,2,1:T(8,128)(2,1)S(1)} %reshape.336, f32[32,128,512]{2,1,0:T(8,128)} %get-tuple-element.158, f32[32,128]{1,0:T(8,128)S(1)} %get-tuple-element.159), kind=kOutput, calls=%fused_computation.18.clone.1 | convolution fusion | flops 71368704 | bytes 9060864 | tf_op jit(solution)/shard_map/while/body/eval_jaxpr/hqk,khd->qhd/dot_general | solution.py:45
  160.6 2.9 gather_fusion.1
  168.5 6.8 %fusion.132 = (f32[32,128]{1,0:T(8,128)S(1)}, f32[32,128,512]{2,1,0:T(8,128)}) fusion(f32[512]{0:T(512)S(1)} %bitcast_convert_fusion.2, bf16[512,32,16]{0,2,1:T(8,128)(2,1)S(1)} %reshape.337, bf16[8,128,32,16]{1,3,2,0:T(8,128)(2,1)} %get-tuple-element.187, s32[]{:T(128)S(6)} %select_n.100), kind=kOutput, calls=%fused_computation.137.clone.1 | convolution fusion | flops 75497984 | bytes 9062404 | tf_op jit(solution)/shard_map/while/body/eval_jaxpr/sub | solution.py:43
  175.8 5.3 %fusion.133 = bf16[8,128,32,16]{1,3,2,0:T(8,128)(2,1)} fusion(bf16[8,128,32,16]{1,3,2,0:T(8,128)(2,1)} %get-tuple-element.172, s32[]{:T(128)} %get-tuple-element.171, bf16[512,32,16]{0,2,1:T(8,128)(2,1)S(1)} %reshape.336, f32[32,128,512]{2,1,0:T(8,128)} %get-tuple-element.158, f32[32,128]{1,0:T(8,128)S(1)} %get-tuple-element.159), kind=kOutput, calls=%fused_computation.18.clone.1 | convolution fusion | flops 71368704 | bytes 9060864 | tf_op jit(solution)/shard_map/while/body/eval_jaxpr/hqk,khd->qhd/dot_general | solution.py:45
  187.2 2.9 gather_fusion.1
  195.1 6.8 %fusion.132 = (f32[32,128]{1,0:T(8,128)S(1)}, f32[32,128,512]{2,1,0:T(8,128)}) fusion(f32[512]{0:T(512)S(1)} %bitcast_convert_fusion.2, bf16[512,32,16]{0,2,1:T(8,128)(2,1)S(1)} %reshape.337, bf16[8,128,32,16]{1,3,2,0:T(8,128)(2,1)} %get-tuple-element.187, s32[]{:T(128)S(6)} %select_n.100), kind=kOutput, calls=%fused_computation.137.clone.1 | convolution fusion | flops 75497984 | bytes 9062404 | tf_op jit(solution)/shard_map/while/body/eval_jaxpr/sub | solution.py:43
  202.4 5.3 %fusion.133 = bf16[8,128,32,16]{1,3,2,0:T(8,128)(2,1)} fusion(bf16[8,128,32,16]{1,3,2,0:T(8,128)(2,1)} %get-tuple-element.172, s32[]{:T(128)} %get-tuple-element.171, bf16[512,32,16]{0,2,1:T(8,128)(2,1)S(1)} %reshape.336, f32[32,128,512]{2,1,0:T(8,128)} %get-tuple-element.158, f32[32,128]{1,0:T(8,128)S(1)} %get-tuple-element.159), kind=kOutput, calls=%fused_computation.18.clone.1 | convolution fusion | flops 71368704 | bytes 9060864 | tf_op jit(solution)/shard_map/while/body/eval_jaxpr/hqk,khd->qhd/dot_general | solution.py:45
  213.8 2.9 gather_fusion.1
  221.7 6.8 %fusion.132 = (f32[32,128]{1,0:T(8,128)S(1)}, f32[32,128,512]{2,1,0:T(8,128)}) fusion(f32[512]{0:T(512)S(1)} %bitcast_convert_fusion.2, bf16[512,32,16]{0,2,1:T(8,128)(2,1)S(1)} %reshape.337, bf16[8,128,32,16]{1,3,2,0:T(8,128)(2,1)} %get-tuple-element.187, s32[]{:T(128)S(6)} %select_n.100), kind=kOutput, calls=%fused_computation.137.clone.1 | convolution fusion | flops 75497984 | bytes 9062404 | tf_op jit(solution)/shard_map/while/body/eval_jaxpr/sub | solution.py:43
  229.0 5.3 %fusion.133 = bf16[8,128,32,16]{1,3,2,0:T(8,128)(2,1)} fusion(bf16[8,128,32,16]{1,3,2,0:T(8,128)(2,1)} %get-tuple-element.172, s32[]{:T(128)} %get-tuple-element.171, bf16[512,32,16]{0,2,1:T(8,128)(2,1)S(1)} %reshape.336, f32[32,128,512]{2,1,0:T(8,128)} %get-tuple-element.158, f32[32,128]{1,0:T(8,128)S(1)} %get-tuple-element.159), kind=kOutput, calls=%fused_computation.18.clone.1 | convolution fusion | flops 71368704 | bytes 9060864 | tf_op jit(solution)/shard_map/while/body/eval_jaxpr/hqk,khd->qhd/dot_general | solution.py:45
  240.4 2.9 gather_fusion.1
  248.3 6.8 %fusion.132 = (f32[32,128]{1,0:T(8,128)S(1)}, f32[32,128,512]{2,1,0:T(8,128)}) fusion(f32[512]{0:T(512)S(1)} %bitcast_convert_fusion.2, bf16[512,32,16]{0,2,1:T(8,128)(2,1)S(1)} %reshape.337, bf16[8,128,32,16]{1,3,2,0:T(8,128)(2,1)} %get-tuple-element.187, s32[]{:T(128)S(6)} %select_n.100), kind=kOutput, calls=%fused_computation.137.clone.1 | convolution fusion | flops 75497984 | bytes 9062404 | tf_op jit(solution)/shard_map/while/body/eval_jaxpr/sub | solution.py:43
  255.6 5.3 %fusion.133 = bf16[8,128,32,16]{1,3,2,0:T(8,128)(2,1)} fusion(bf16[8,128,32,16]{1,3,2,0:T(8,128)(2,1)} %get-tuple-element.172, s32[]{:T(128)} %get-tuple-element.171, bf16[512,32,16]{0,2,1:T(8,128)(2,1)S(1)} %reshape.336, f32[32,128,512]{2,1,0:T(8,128)} %get-tuple-element.158, f32[32,128]{1,0:T(8,128)S(1)} %get-tuple-element.159), kind=kOutput, calls=%fused_computation.18.clone.1 | convolution fusion | flops 71368704 | bytes 9060864 | tf_op jit(solution)/shard_map/while/body/eval_jaxpr/hqk,khd->qhd/dot_general | solution.py:45
  267.2 24.3 %select_convert_fusion = bf16[1024,512]{0,1:T(8,128)(2,1)S(1)} fusion(f32[1024,512]{0,1:T(8,128)} %copy-done.2, bf16[2048,512]{1,0:T(8,128)(2,1)S(1)} %copy-done, bf16[512,2048]{1,0:T(8,128)(2,1)} %param.24, f32[512]{0:T(512)S(1)} %copy-done.5, f32[1024]{0:T(1024)S(1)} %add_rsqrt_fusion, f32[1024]{0:T(1024)S(1)} %broadcast_multiply_fusion, ...), kind=kOutput, calls=%fused_computation.68 | convolution fusion | flops 4434952192 | bytes 7351296 | tf_op jit(solution)/shard_map/dot_general | solution.py:109
  (165 shorter events, 112.5 us)
Async XLA Ops:
  0.0 267.2 %copy-start = (bf16[2048,512]{1,0:T(8,128)(2,1)S(1)}, bf16[2048,512]{1,0:T(8,128)(2,1)}, u32[]{:S(2)}) copy-start(bf16[2048,512]{1,0:T(8,128)(2,1)} %param.25) | copy-start | bytes 6291460
  0.0 6.4 %copy-start.4 = (s32[1,2,3]{2,1,0:T(2,128)S(1)}, s32[1,2,3]{2,1,0:T(2,128)}, u32[]{:S(2)}) copy-start(s32[1,2,3]{2,1,0:T(2,128)} %param.17) | copy-start | bytes 76
  1.7 32.9 %copy-start.1 = (bf16[1024,512]{0,1:T(8,128)(2,1)}, bf16[1024,512]{0,1:T(8,128)(2,1)S(1)}, u32[]{:S(2)}) copy-start(bf16[1024,512]{0,1:T(8,128)(2,1)S(1)} %copy.21) | copy-start | bytes 3145732
  9.0 29.9 %collective-permute-start = (bf16[3,128,512]{2,1,0:T(8,128)(2,1)}, bf16[3,128,512]{2,1,0:T(8,128)(2,1)S(1)}, u32[]{:S(2)}, u32[]{:S(2)}) collective-permute-start(bf16[3,128,512]{2,1,0:T(8,128)(2,1)} %gather_fusion.3), channel_id=1, source_target_pairs={{0,1},{1,2},{2,3},{3,4},{4,5},{5,6},{6,7},{7,8},{8,9},{9,10},{10,1... | collective-permute-start | bytes 1179656 | tf_op jit(solution)/shard_map/ppermute | solution.py:14
  15.3 22.8 %copy-start.3 = (s32[8,3]{0,1:T(4,128)S(1)}, s32[8,3]{0,1:T(4,128)}, u32[]{:S(2)}) copy-start(s32[8,3]{0,1:T(4,128)} %param.18) | copy-start | bytes 292
  15.3 26.4 %collective-permute-start.1 = (bf16[3,128,512]{2,1,0:T(8,128)(2,1)}, bf16[3,128,512]{2,1,0:T(8,128)(2,1)}, u32[]{:S(2)}, u32[]{:S(2)}) collective-permute-start(bf16[3,128,512]{2,1,0:T(8,128)(2,1)} %gather_fusion.4), channel_id=1, source_target_pairs={{1,0},{2,1},{3,2},{4,3},{5,4},{6,5},{7,6},{8,7},{9,8},{10,9},{11,1... | collective-permute-start | bytes 1179656 | tf_op jit(solution)/shard_map/ppermute | solution.py:14
  19.1 19.0 %collective-permute-start.2 = (bf16[3,128]{1,0:T(4,128)(2,1)}, bf16[3,128]{1,0:T(4,128)(2,1)}, u32[]{:S(2)}, u32[]{:S(2)}) collective-permute-start(bf16[3,128]{1,0:T(4,128)(2,1)} %gather_fusion.5), channel_id=1, source_target_pairs={{0,1},{1,2},{2,3},{3,4},{4,5},{5,6},{6,7},{7,8},{8,9},{9,10},{10,1... | collective-permute-start | bytes 2312 | tf_op jit(solution)/shard_map/ppermute | solution.py:14
  23.3 14.8 %collective-permute-start.3 = (bf16[3,128]{1,0:T(4,128)(2,1)S(1)}, bf16[3,128]{1,0:T(4,128)(2,1)}, u32[]{:S(2)}, u32[]{:S(2)}) collective-permute-start(bf16[3,128]{1,0:T(4,128)(2,1)S(1)} %gather_fusion.6), channel_id=1, source_target_pairs={{1,0},{2,1},{3,2},{4,3},{5,4},{6,5},{7,6},{8,7},{9,8},{10,9},{11,1... | collective-permute-start | bytes 2312 | tf_op jit(solution)/shard_map/ppermute | solution.py:14
  260.9 6.3 %copy-start.5 = (f32[512]{0:T(512)S(1)}, f32[512]{0:T(512)}, u32[]{:S(2)}) copy-start(f32[512]{0:T(512)} %param.23) | copy-start | bytes 6148
  260.9 6.3 %copy-start.6 = (pred[1024]{0:T(1024)(128)(4,1)S(1)}, pred[1024]{0:T(1024)(128)(4,1)}, u32[]{:S(2)}) copy-start(pred[1024]{0:T(1024)(128)(4,1)} %iota_compare_fusion) | copy-start | bytes 3076
  265.5 1.3 copy-start.2
where the time goes:
time: 297 us; the launch traced here: 293 us
  matrix products  138 us (46%)
  local copies, waits for them, and re-layouts  96.4 us (32%)
  other arithmetic  30.3 us (10%)
  loops' own time  15.5 us (5%)
  starting transfers between devices  11.3 us (4%)
    sub x8, matrix products, one_block(): expo = jnp.exp(scores - top)  54.2 us
    dot_general x8, matrix products, one_block(): jnp.einsum('hqk,khd->qhd', weights, value_rows, preferred_element_type=jn...  42.6 us
    dot_general x1, matrix products, on_device(): jnp.dot(hidden, down_weight, preferred_element_type=jnp.float32)  24.3 us
    gather x8, local copies, waits for them, and re-layouts, one_block(): jnp.take(pool_values, chosen, axis=0).reshape(-1, heads, head_size)  22.9 us
    gather x8, local copies, waits for them, and re-layouts, one_block(): key_rows = jnp.take(pool_keys, chosen, axis=0).reshape(-1, heads, head_size)  22.9 us
    another operation x1, loops' own time, attend_blocks(): return lax.map(one_block, jnp.arange(queries.shape[0], dtype=jnp.int32))  15.5 us
    ppermute x4, starting transfers between devices, passed_along(): return lax.ppermute(array, axis, pairs)  11.3 us
    select_n x8, other arithmetic, one_block(): key_rows = jnp.take(pool_keys, chosen, axis=0).reshape(-1, heads, head_size)  10.9 us
  transfers between devices with their start and end apart: 4, of which 0 were waited for; matrix products, arithmetic and copies ran while one was open for 7% of the time, Pallas kernels for 0%

commit v1 on v0

v1 whole, which is shorter than its diff:
```python
import functools
import math

import jax
import jax.numpy as jnp
from jax import lax
from jax.experimental import pallas as pl
from jax.experimental.pallas import tpu as pltpu
from jax.sharding import PartitionSpec as P

H = 32
LANES = 128
MARK = 1000.0
NEG = -1000000000.0
LOG2E = 1.4426950408889634
STACK = 4


def passed_along(array, axis, by):
    count = lax.axis_size(axis)
    pairs = [(i, i + by) for i in range(count) if 0 <= i + by < count]
    return lax.ppermute(array, axis, pairs)


def layer_norm(inputs, gain):
    center = inputs - jnp.mean(inputs, axis=-1, keepdims=True)
    spread = jnp.mean(center * center, axis=-1, keepdims=True)
    return center * lax.rsqrt(spread + 1e-05) * gain


def pack_kernel(send_ref, length_ref, first_ref, second_ref, right_ref, left_ref):
    step = pl.program_id(0)
    rows = first_ref.shape[0]
    for block, source, target in (
        (send_ref[1, step], first_ref, right_ref),
        (send_ref[0, step], second_ref, left_ref),
    ):
        position = block * rows + lax.broadcasted_iota(jnp.int32, source.shape, 0)
        value = source[...].astype(jnp.float32)
        target[...] = jnp.where(position < length_ref[0], value, MARK).astype(target.dtype)


def pack(points, send, lengths, block_rows):
    width = points.shape[1]
    count = send.shape[1]
    shape = jax.ShapeDtypeStruct((count * block_rows, width), points.dtype)
    return pl.pallas_call(
        pack_kernel,
        out_shape=(shape, shape),
        grid_spec=pltpu.PrefetchScalarGridSpec(
            num_scalar_prefetch=2,
            grid=(count,),
            in_specs=[
                pl.BlockSpec((block_rows, width), lambda s, send, _: (send[1, s], 0)),
                pl.BlockSpec((block_rows, width), lambda s, send, _: (send[0, s], 0)),
            ],
            out_specs=[
                pl.BlockSpec((block_rows, width), lambda s, send, _: (s, 0)),
                pl.BlockSpec((block_rows, width), lambda s, send, _: (s, 0)),
            ],
        ),
        name="pack",
    )(send, lengths, points, points)


def project_kernel(scale, x_ref, gain_ref, qk_ref, v_ref, q_out, k_out, v_out):
    normed = layer_norm(x_ref[...].astype(jnp.float32), gain_ref[...]).astype(jnp.bfloat16)
    queries = jnp.dot(normed, qk_ref[0], preferred_element_type=jnp.float32)
    q_out[...] = (queries * scale).astype(q_out.dtype)
    k_out[...] = jnp.dot(normed, qk_ref[1], preferred_element_type=jnp.float32).astype(k_out.dtype)
    v_out[...] = jnp.dot(normed, v_ref[...], preferred_element_type=jnp.float32).astype(v_out.dtype)


def project(points, gain, qk_weight, v_weight, scale, tile=256):
    rows, width = points.shape
    shape = jax.ShapeDtypeStruct((rows, width), jnp.bfloat16)
    row_spec = pl.BlockSpec((tile, width), lambda i: (i, 0))
    return pl.pallas_call(
        functools.partial(project_kernel, scale),
        out_shape=(shape, shape, shape),
        grid=(rows // tile,),
        in_specs=[
            row_spec,
            pl.BlockSpec(gain.shape, lambda i: (0, 0)),
            pl.BlockSpec(qk_weight.shape, lambda i: (0, 0, 0)),
            pl.BlockSpec(v_weight.shape, lambda i: (0, 0)),
        ],
        out_specs=[row_spec] * 3,
        cost_estimate=pl.CostEstimate(
            flops=6 * rows * width * width,
            bytes_accessed=8 * rows * width + 6 * width * width,
            transcendentals=0,
        ),
        name="project",
    )(points, gain, qk_weight, v_weight)


def attend_kernel(
    block_rows,
    head_size,
    pattern_ref,
    length_ref,
    q_ref,
    k_ref,
    v_ref,
    left_ref,
    right_ref,
    gain_ref,
    wk_ref,
    wv_ref,
    out_ref,
    k_pool,
    v_pool,
    b_pool,
):
    step = pl.program_id(0)
    local, width = k_ref.shape
    offered = left_ref.shape[0]
    per_tile = LANES // head_size
    first_lane = lambda shape: lax.broadcasted_iota(jnp.int32, shape, 1) == 0

    @pl.when(step == 0)
    def _():
        k_pool[0:local, :] = k_ref[...]
        v_pool[0:local, :] = v_ref[...]
        position = lax.broadcasted_iota(jnp.int32, (local, LANES), 0)
        dead = (position >= length_ref[0]) & first_lane((local, LANES))
        b_pool[0:local, :] = jnp.where(dead, NEG, 0.0).astype(b_pool.dtype)
        for index, source in enumerate((left_ref, right_ref)):
            start = local + index * offered
            rows = source[...].astype(jnp.float32)
            normed = layer_norm(rows, gain_ref[...]).astype(jnp.bfloat16)
            k_pool[start : start + offered, :] = jnp.dot(
                normed, wk_ref[0], preferred_element_type=jnp.float32
            ).astype(k_pool.dtype)
            v_pool[start : start + offered, :] = jnp.dot(
                normed, wv_ref[...], preferred_element_type=jnp.float32
            ).astype(v_pool.dtype)
            dead = (rows[:, 0:LANES] > 0.5 * MARK) & first_lane((offered, LANES))
            b_pool[start : start + offered, :] = jnp.where(dead, NEG, 0.0).astype(b_pool.dtype)

    slots = [step] + [pattern_ref[step, s] for s in range(pattern_ref.shape[1])]
    starts = [pl.multiple_of(slot * block_rows, block_rows) for slot in slots]
    lane = lax.broadcasted_iota(jnp.int32, (block_rows, LANES), 1)
    unit = jnp.where(lane == 0, 1.0, 0.0).astype(jnp.bfloat16)
    bias = jnp.concatenate([b_pool[pl.ds(start, block_rows), :] for start in starts], axis=0)
    ones = jnp.ones((len(slots) * block_rows, LANES), jnp.bfloat16)

    for tile in range(width // LANES):
        columns = pl.ds(tile * LANES, LANES)
        keys = jnp.concatenate(
            [k_pool[pl.ds(start, block_rows), columns] for start in starts], axis=0
        )
        values = jnp.concatenate(
            [v_pool[pl.ds(start, block_rows), columns] for start in starts], axis=0
        )
        keys = jnp.concatenate([keys, bias], axis=1)
        values = jnp.concatenate([values, ones], axis=1)
        queries = q_ref[:, columns].astype(jnp.float32)
        top = bottom = None
        for group in range(0, per_tile, STACK):
            heads = range(group, group + STACK)
            stacked = jnp.concatenate(
                [
                    jnp.concatenate(
                        [
                            jnp.where(lane // head_size == head, queries, 0.0).astype(jnp.bfloat16),
                            unit,
                        ],
                        axis=1,
                    )
                    for head in heads
                ],
                axis=0,
            )
            scores = lax.dot_general(
                stacked, keys, (((1,), (1,)), ((), ())), preferred_element_type=jnp.float32
            )
            expo = jnp.exp2(scores - jnp.max(scores, axis=-1, keepdims=True)).astype(jnp.bfloat16)
            mixed = jnp.dot(expo, values, preferred_element_type=jnp.float32)
            for index, head in enumerate(heads):
                part = mixed[index * block_rows : (index + 1) * block_rows]
                num, den = part[:, :LANES], part[:, LANES:]
                if top is None:
                    top, bottom = num, den
                else:
                    mine = lane // head_size == head
                    top = jnp.where(mine, num, top)
                    bottom = jnp.where(mine, den, bottom)
        out_ref[:, columns] = (top / bottom).astype(out_ref.dtype)


def attend(queries, keys, values, left, right, pattern, lengths, gain, qk_weight, v_weight):
    rows, width = queries.shape
    blocks = pattern.shape[0]
    block_rows = rows // blocks
    pool = rows + left.shape[0] + right.shape[0]
    row_spec = pl.BlockSpec((block_rows, width), lambda i, *_: (i, 0))
    whole = lambda shape: pl.BlockSpec(shape, lambda i, *_: (0,) * len(shape))
    return pl.pallas_call(
        functools.partial(attend_kernel, block_rows, width // H),
        out_shape=jax.ShapeDtypeStruct((rows, width), jnp.bfloat16),
        grid_spec=pltpu.PrefetchScalarGridSpec(
            num_scalar_prefetch=2,
            grid=(blocks,),
            in_specs=[
                row_spec,
                whole(keys.shape),
                whole(values.shape),
                whole(left.shape),
                whole(right.shape),
                whole(gain.shape),
                pl.BlockSpec((1, width, width), lambda i, *_: (1, 0, 0)),
                whole(v_weight.shape),
            ],
            out_specs=row_spec,
            scratch_shapes=[
                pltpu.VMEM((pool, width), jnp.bfloat16),
                pltpu.VMEM((pool, width), jnp.bfloat16),
                pltpu.VMEM((pool, LANES), jnp.bfloat16),
            ],
        ),
        compiler_params=pltpu.CompilerParams(vmem_limit_bytes=48 << 20),
        name="attend",
    )(pattern, lengths, queries, keys, values, left, right, gain, qk_weight, v_weight)


def mix_kernel(length_ref, x_ref, a_ref, wo_ref, gain_ref, up_ref, down_ref, out_ref):
    rows = x_ref.shape[0]
    mixed = x_ref[...].astype(jnp.float32) + jnp.dot(
        a_ref[...], wo_ref[...], preferred_element_type=jnp.float32
    )
    normed = layer_norm(mixed, gain_ref[...]).astype(jnp.bfloat16)
    inner = jnp.dot(normed, up_ref[...], preferred_element_type=jnp.float32)
    hidden = (0.5 * inner * (1.0 + lax.erf(inner * math.sqrt(0.5)))).astype(jnp.bfloat16)
    result = mixed + jnp.dot(hidden, down_ref[...], preferred_element_type=jnp.float32)
    position = pl.program_id(0) * rows + lax.broadcasted_iota(jnp.int32, result.shape, 0)
    out_ref[...] = jnp.where(position < length_ref[0], result, 0.0).astype(out_ref.dtype)


def mix(points, attended, lengths, o_weight, gain, up_weight, down_weight, tile=256):
    rows, width = points.shape
    row_spec = pl.BlockSpec((tile, width), lambda i, *_: (i, 0))
    whole = lambda shape: pl.BlockSpec(shape, lambda i, *_: (0,) * len(shape))
    return pl.pallas_call(
        mix_kernel,
        out_shape=jax.ShapeDtypeStruct((rows, width), jnp.bfloat16),
        grid_spec=pltpu.PrefetchScalarGridSpec(
            num_scalar_prefetch=1,
            grid=(rows // tile,),
            in_specs=[
                row_spec,
                row_spec,
                whole(o_weight.shape),
                whole(gain.shape),
                whole(up_weight.shape),
                whole(down_weight.shape),
            ],
            out_specs=row_spec,
        ),
        compiler_params=pltpu.CompilerParams(vmem_limit_bytes=48 << 20),
        name="mix",
    )(lengths, points, attended, o_weight, gain, up_weight, down_weight)


def on_device(
    points,
    lengths,
    send_blocks,
    pattern,
    ln1_gain,
    qk_weight,
    v_weight,
    o_weight,
    ln2_gain,
    up_weight,
    down_weight,
):
    rows, width = points.shape
    block_rows = rows // pattern.shape[0]
    gain1, gain2 = ln1_gain[None, :], ln2_gain[None, :]
    to_right, to_left = pack(points, send_blocks[0], lengths, block_rows)
    left = passed_along(to_right, "patch", 1)
    right = passed_along(to_left, "patch", -1)
    scale = LOG2E / math.sqrt(width // H)
    queries, keys, values = project(points, gain1, qk_weight, v_weight, scale)
    attended = attend(
        queries, keys, values, left, right, pattern, lengths, gain1, qk_weight, v_weight
    )
    return mix(points, attended, lengths, o_weight, gain2, up_weight, down_weight)


def solution(mesh):
    in_specs = (
        P(("groups", "patch"), None),
        P(("groups", "patch")),
        P(("groups", "patch"), None, None),
        P(("groups", "patch"), None),
        P(),
        P(),
        P(),
        P(),
        P(),
        P(),
        P(),
    )
    out_specs = P(("groups", "patch"), None)
    return jax.shard_map(
        on_device, mesh=mesh, in_specs=in_specs, out_specs=out_specs, check_vma=False
    )
```

time: 297 us -> 58.6 us (0.20); the launches traced: 293 us -> 58.2 us
  matrix products: 138 us -> 0 us
  local copies, waits for them, and re-layouts: 96.4 us -> 3.78 us
  Pallas kernels: 0 us -> 45 us
  other arithmetic: 30.3 us -> 0 us
  loops' own time: 15.5 us -> 0 us
  starting transfers between devices: 11.3 us -> 5.62 us
  waiting for transfers between devices: 0.01 us -> 3.03 us
    dot_general x17 -> x0, matrix products: 84.2 us -> none  [the longest x8 42.6 us: one_block(): jnp.einsum('hqk,khd->qhd', weights, value_rows, preferred_element_type=jn...]
    gather x28 -> x0, local copies, waits for them, and re-layouts: 57.1 us -> none  [the longest x8 22.9 us: one_block(): jnp.take(pool_values, chosen, axis=0).reshape(-1, heads, head_size)]
    sub x8 -> x0, matrix products: 54.2 us -> none  [one_block(): expo = jnp.exp(scores - top)]
    pallas_call x0 -> x4, Pallas kernels: none -> 45 us  [the longest x1 26.2 us: attend(): pl.pallas_call(functools.partial(attend_kernel, block_rows, width // H),...]
    select_n x17 -> x0, other arithmetic: 16.5 us -> none  [the longest x8 10.9 us: one_block(): key_rows = jnp.take(pool_keys, chosen, axis=0).reshape(-1, heads, head_size)]
    another operation x1 -> x0, loops' own time: 15.5 us -> none  [attend_blocks(): return lax.map(one_block, jnp.arange(queries.shape[0], dtype=jnp.int32))]
    reshape x17 -> x0, local copies, waits for them, and re-layouts: 13.8 us -> none  [the longest x8 9.91 us: one_block(): key_rows = jnp.take(pool_keys, chosen, axis=0).reshape(-1, heads, head_size)]
    select_n x16 -> x0, local copies, waits for them, and re-layouts: 10.9 us -> none  [the longest x8 8.39 us: one_block(): key_rows = jnp.take(pool_keys, chosen, axis=0).reshape(-1, heads, head_size)]
  transfers between devices with their start and end apart: 4 -> 2, of which waited for: 0 -> 1; matrix products, arithmetic and copies ran while one was open for 7% -> 0% of each run, Pallas kernels for 0% -> 10%
where the time goes in v1:
time: 58.6 us; the launch traced here: 58.2 us
  Pallas kernels  45 us (77%)
  starting transfers between devices  5.62 us (10%)
  local copies, waits for them, and re-layouts  3.78 us (6%)
  waiting for transfers between devices  3.03 us (5%)
  between operations  0.74 us (1%)
    pallas_call x1, Pallas kernels, attend(): pl.pallas_call(functools.partial(attend_kernel, block_rows, width // H),...  26.2 us
    pallas_call x1, Pallas kernels, mix(): pl.pallas_call(mix_kernel, out_shape=jax.ShapeDtypeStruct((rows, width),...  9.47 us
    pallas_call x1, Pallas kernels, project(): pl.pallas_call(functools.partial(project_kernel, scale), out_shape=(shape...  5.63 us
    ppermute x2, starting transfers between devices, passed_along(): return lax.ppermute(array, axis, pairs)  5.62 us
    unnamed x21, local copies, waits for them, and re-layouts  3.78 us
    pallas_call x1, Pallas kernels, pack(): pl.pallas_call(pack_kernel, out_shape=(shape, shape), grid_spec=pltpu.Pre...  3.63 us
    ppermute x2, waiting for transfers between devices, passed_along(): return lax.ppermute(array, axis, pairs)  3.03 us
  transfers between devices with their start and end apart: 2, of which 1 were waited for; matrix products, arithmetic and copies ran while one was open for 0% of the time, Pallas kernels for 10%

profile of v1, /device:TPU:25, one launch (start us, length us, event | category | flops | bytes accessed | tf_op | source)
XLA Modules:
  0.0 58.2 jit_solution(14158375915457641028)
XLA Ops:
  0.0 0.0 copy-start.9
  0.7 3.6 %pack.1 = (bf16[384,512]{1,0:T(8,128)(2,1)}, bf16[384,512]{1,0:T(8,128)(2,1)}) custom-call(s32[2,3]{1,0:T(2,128)} %bitcast.6, s32[1]{0:T(128)S(6)} %copy.13.length_ref, bf16[1024,512]{1,0:T(8,128)(2,1)} %x_ref.3, bf16[1024,512]{1,0:T(8,128)(2,1)} %x_ref.3), custom_call_target="tpu_custom_call" | custom-call | tf_op jit(solution)/shard_map/pack/pallas_call | solution.py:47
  4.3 3.7 %collective-permute-start = (bf16[384,512]{1,0:T(8,128)(2,1)}, bf16[384,512]{1,0:T(8,128)(2,1)S(1)}, u32[]{:S(2)}, u32[]{:S(2)}) collective-permute-start(bf16[384,512]{1,0:T(8,128)(2,1)} %get-tuple-element.13), channel_id=1, source_target_pairs={{0,1},{1,2},{2,3},{3,4},{4,5},{5,6},{6,7},{7,8},{8,9},{9,10},{10,1... | collective-permute-start | bytes 1179656 | tf_op jit(solution)/shard_map/ppermute | solution.py:22
  8.0 1.9 %collective-permute-start.1 = (bf16[384,512]{1,0:T(8,128)(2,1)}, bf16[384,512]{1,0:T(8,128)(2,1)S(1)}, u32[]{:S(2)}, u32[]{:S(2)}) collective-permute-start(bf16[384,512]{1,0:T(8,128)(2,1)} %get-tuple-element.14), channel_id=1, source_target_pairs={{1,0},{2,1},{3,2},{4,3},{5,4},{6,5},{7,6},{8,7},{9,8},{10,9},{11,1... | collective-permute-start | bytes 1179656 | tf_op jit(solution)/shard_map/ppermute | solution.py:22
  9.9 0.0 copy-done.9
  9.9 0.1 copy.12.pattern_ref
  10.0 0.0 copy-start.6
  10.0 0.0 copy-start.7
  10.0 5.6 %project.1 = (bf16[1024,512]{1,0:T(8,128)(2,1)}, bf16[1024,512]{1,0:T(8,128)(2,1)}, bf16[1024,512]{1,0:T(8,128)(2,1)}) custom-call(bf16[1024,512]{1,0:T(8,128)(2,1)} %x_ref.3, f32[1,512]{1,0:T(1,128)} %bitcast.3, bf16[2,512,512]{2,1,0:T(8,128)(2,1)} %wk_ref.1, bf16[512,512]{1,0:T(8,128)(2,1)} %wv_ref.1), custom_call_target="tpu_custom_call" | custom-call | flops 1610612736 | bytes 5767168 | tf_op jit(solution)/shard_map/project/pallas_call | solution.py:78
  15.7 0.0 collective-permute-done.left_ref
  15.7 3.0 %collective-permute-done.1.right_ref = bf16[384,512]{1,0:T(8,128)(2,1)S(1)} collective-permute-done((bf16[384,512]{1,0:T(8,128)(2,1)}, bf16[384,512]{1,0:T(8,128)(2,1)S(1)}, u32[]{:S(2)}, u32[]{:S(2)}) %collective-permute-start.1) | collective-permute-done | bytes 393248 | tf_op jit(solution)/shard_map/ppermute | solution.py:22
  18.7 0.0 copy-done.6
  18.7 0.0 copy-done.7
  18.7 0.0 copy-start.2
  18.7 1.2 %copy-done.2 = bf16[1024,512]{1,0:T(8,128)(2,1)S(1)} copy-done((bf16[1024,512]{1,0:T(8,128)(2,1)S(1)}, bf16[1024,512]{1,0:T(8,128)(2,1)}, u32[]{:S(2)}) %copy-start.2) | copy-done | bytes 1048600
  19.9 0.0 copy-start.3
  19.9 1.2 %copy-done.3 = bf16[1024,512]{1,0:T(8,128)(2,1)S(1)} copy-done((bf16[1024,512]{1,0:T(8,128)(2,1)S(1)}, bf16[1024,512]{1,0:T(8,128)(2,1)}, u32[]{:S(2)}) %copy-start.3) | copy-done | bytes 1048600
  21.2 0.0 copy-start.4
  21.2 1.2 %copy-done.4 = bf16[1024,512]{1,0:T(8,128)(2,1)S(1)} copy-done((bf16[1024,512]{1,0:T(8,128)(2,1)S(1)}, bf16[1024,512]{1,0:T(8,128)(2,1)}, u32[]{:S(2)}) %copy-start.4) | copy-done | bytes 1048600
  22.4 0.0 copy-start
  22.4 0.0 copy-start.1
  22.4 0.0 copy-start.5
  22.4 0.0 copy-start.8
  22.4 26.2 %attend.1.a_ref = bf16[1024,512]{1,0:T(8,128)(2,1)S(1)} custom-call(s32[8,3]{1,0:T(8,128)S(1)} %copy.12.pattern_ref, s32[1]{0:T(128)S(6)} %copy.13.length_ref, bf16[1024,512]{1,0:T(8,128)(2,1)S(1)} %copy-done.2, bf16[1024,512]{1,0:T(8,128)(2,1)S(1)} %copy-done.3, bf16[1024,512]{1,0:T(8,128)(2,1)S(1)} %copy-done.4, ...), custom_call_target="tpu_custom_call" | custom-call | tf_op jit(solution)/shard_map/attend/pallas_call | solution.py:200
  48.6 0.0 copy-done
  48.7 0.0 copy-done.1
  48.7 0.0 copy-done.5
  48.7 0.0 copy-done.8
  48.7 9.5 %mix.1 = bf16[1024,512]{1,0:T(8,128)(2,1)} custom-call(s32[1]{0:T(128)S(6)} %copy.13.length_ref, bf16[1024,512]{1,0:T(8,128)(2,1)S(1)} %copy-done, bf16[1024,512]{1,0:T(8,128)(2,1)S(1)} %attend.1.a_ref, bf16[512,512]{1,0:T(8,128)(2,1)S(1)} %copy-done.5, f32[1,512]{1,0:T(1,128)S(1)} %bitcast.5, bf16[512,2048]{1,0:T(8,128)(2,1)S(1)} %copy-done.1, ...), custom_call_target="tpu_custom_call" | custom-call | tf_op jit(solution)/shard_map/mix/pallas_call | solution.py:245
Async XLA Ops:
  0.0 9.9 %copy-start.9 = (s32[8,3]{0,1:T(4,128)S(1)}, s32[8,3]{0,1:T(4,128)}, u32[]{:S(2)}) copy-start(s32[8,3]{0,1:T(4,128)} %param.14) | copy-start | bytes 292
  4.3 11.4 %collective-permute-start = (bf16[384,512]{1,0:T(8,128)(2,1)}, bf16[384,512]{1,0:T(8,128)(2,1)S(1)}, u32[]{:S(2)}, u32[]{:S(2)}) collective-permute-start(bf16[384,512]{1,0:T(8,128)(2,1)} %get-tuple-element.13), channel_id=1, source_target_pairs={{0,1},{1,2},{2,3},{3,4},{4,5},{5,6},{6,7},{7,8},{8,9},{9,10},{10,1... | collective-permute-start | bytes 1179656 | tf_op jit(solution)/shard_map/ppermute | solution.py:22
  8.0 10.7 %collective-permute-start.1 = (bf16[384,512]{1,0:T(8,128)(2,1)}, bf16[384,512]{1,0:T(8,128)(2,1)S(1)}, u32[]{:S(2)}, u32[]{:S(2)}) collective-permute-start(bf16[384,512]{1,0:T(8,128)(2,1)} %get-tuple-element.14), channel_id=1, source_target_pairs={{1,0},{2,1},{3,2},{4,3},{5,4},{6,5},{7,6},{8,7},{9,8},{10,9},{11,1... | collective-permute-start | bytes 1179656 | tf_op jit(solution)/shard_map/ppermute | solution.py:22
  10.0 8.7 %copy-start.6 = (bf16[512,512]{1,0:T(8,128)(2,1)S(1)}, bf16[512,512]{1,0:T(8,128)(2,1)}, u32[]{:S(2)}) copy-start(bf16[512,512]{1,0:T(8,128)(2,1)} %wv_ref.1) | copy-start | bytes 1572868
  10.0 8.7 %copy-start.7 = (f32[512]{0:T(512)S(1)}, f32[512]{0:T(512)}, u32[]{:S(2)}) copy-start(f32[512]{0:T(512)} %param.15) | copy-start | bytes 6148
  18.7 1.2 %copy-start.2 = (bf16[1024,512]{1,0:T(8,128)(2,1)S(1)}, bf16[1024,512]{1,0:T(8,128)(2,1)}, u32[]{:S(2)}) copy-start(bf16[1024,512]{1,0:T(8,128)(2,1)} %get-tuple-element.10.q_ref) | copy-start | bytes 3145732
  19.9 1.2 %copy-start.3 = (bf16[1024,512]{1,0:T(8,128)(2,1)S(1)}, bf16[1024,512]{1,0:T(8,128)(2,1)}, u32[]{:S(2)}) copy-start(bf16[1024,512]{1,0:T(8,128)(2,1)} %get-tuple-element.11.k_ref) | copy-start | bytes 3145732
  21.2 1.2 %copy-start.4 = (bf16[1024,512]{1,0:T(8,128)(2,1)S(1)}, bf16[1024,512]{1,0:T(8,128)(2,1)}, u32[]{:S(2)}) copy-start(bf16[1024,512]{1,0:T(8,128)(2,1)} %get-tuple-element.12.v_ref) | copy-start | bytes 3145732
  22.4 26.3 %copy-start = (bf16[1024,512]{1,0:T(8,128)(2,1)S(1)}, bf16[1024,512]{1,0:T(8,128)(2,1)}, u32[]{:S(2)}) copy-start(bf16[1024,512]{1,0:T(8,128)(2,1)} %x_ref.3) | copy-start | bytes 3145732
  22.4 26.3 %copy-start.1 = (bf16[512,2048]{1,0:T(8,128)(2,1)S(1)}, bf16[512,2048]{1,0:T(8,128)(2,1)}, u32[]{:S(2)}) copy-start(bf16[512,2048]{1,0:T(8,128)(2,1)} %up_ref.1) | copy-start | bytes 6291460
  22.4 26.3 %copy-start.5 = (bf16[512,512]{1,0:T(8,128)(2,1)S(1)}, bf16[512,512]{1,0:T(8,128)(2,1)}, u32[]{:S(2)}) copy-start(bf16[512,512]{1,0:T(8,128)(2,1)} %wo_ref.1) | copy-start | bytes 1572868
  22.4 26.3 %copy-start.8 = (f32[512]{0:T(512)S(1)}, f32[512]{0:T(512)}, u32[]{:S(2)}) copy-start(f32[512]{0:T(512)} %param.19) | copy-start | bytes 6148

commit v2 on v1

--- a/solution.py
+++ b/solution.py
@@ -13,7 +13,7 @@
 MARK = 1000.0
 NEG = -1000000000.0
 LOG2E = 1.4426950408889634
-STACK = 4
+STACK = 2
 
 
 def passed_along(array, axis, by):
@@ -28,39 +28,39 @@
     return center * lax.rsqrt(spread + 1e-05) * gain
 
 
-def pack_kernel(send_ref, length_ref, first_ref, second_ref, right_ref, left_ref):
-    step = pl.program_id(0)
-    rows = first_ref.shape[0]
-    for block, source, target in (
-        (send_ref[1, step], first_ref, right_ref),
-        (send_ref[0, step], second_ref, left_ref),
-    ):
-        position = block * rows + lax.broadcasted_iota(jnp.int32, source.shape, 0)
-        value = source[...].astype(jnp.float32)
-        target[...] = jnp.where(position < length_ref[0], value, MARK).astype(target.dtype)
+def pack_kernel(send_ref, length_ref, *refs):
+    sources, targets = refs[:-2], refs[-2:]
+    sides, count = send_ref.shape
+    rows = sources[0].shape[0]
+    for side in range(sides):
+        for slot in range(count):
+            source = sources[side * count + slot]
+            position = send_ref[side, slot] * rows + lax.broadcasted_iota(
+                jnp.int32, source.shape, 0
+            )
+            value = jnp.where(position < length_ref[0], source[...].astype(jnp.float32), MARK)
+            targets[side][slot * rows : (slot + 1) * rows, :] = value.astype(source.dtype)
 
 
 def pack(points, send, lengths, block_rows):
     width = points.shape[1]
-    count = send.shape[1]
+    sides, count = send.shape
     shape = jax.ShapeDtypeStruct((count * block_rows, width), points.dtype)
+
+    def picked(side, slot):
+        return pl.BlockSpec((block_rows, width), lambda i, send, _: (send[side, slot], 0))
+
     return pl.pallas_call(
         pack_kernel,
         out_shape=(shape, shape),
         grid_spec=pltpu.PrefetchScalarGridSpec(
             num_scalar_prefetch=2,
-            grid=(count,),
-            in_specs=[
-                pl.BlockSpec((block_rows, width), lambda s, send, _: (send[1, s], 0)),
-                pl.BlockSpec((block_rows, width), lambda s, send, _: (send[0, s], 0)),
-            ],
-            out_specs=[
-                pl.BlockSpec((block_rows, width), lambda s, send, _: (s, 0)),
-                pl.BlockSpec((block_rows, width), lambda s, send, _: (s, 0)),
-            ],
+            grid=(1,),
+            in_specs=[picked(side, slot) for side in range(sides) for slot in range(count)],
+            out_specs=[pl.BlockSpec(shape.shape, lambda i, *_: (0, 0))] * 2,
         ),
         name="pack",
-    )(send, lengths, points, points)
+    )(send, lengths, *([points] * (sides * count)))
 
 
 def project_kernel(scale, x_ref, gain_ref, qk_ref, v_ref, q_out, k_out, v_out):
@@ -91,6 +91,7 @@
             bytes_accessed=8 * rows * width + 6 * width * width,
             transcendentals=0,
         ),
+        compiler_params=pltpu.CompilerParams(vmem_limit_bytes=16 << 20),
         name="project",
     )(points, gain, qk_weight, v_weight)
 
@@ -220,7 +221,7 @@
                 pltpu.VMEM((pool, LANES), jnp.bfloat16),
             ],
         ),
-        compiler_params=pltpu.CompilerParams(vmem_limit_bytes=48 << 20),
+        compiler_params=pltpu.CompilerParams(vmem_limit_bytes=24 << 20),
         name="attend",
     )(pattern, lengths, queries, keys, values, left, right, gain, qk_weight, v_weight)
 
@@ -258,7 +259,7 @@
             ],
             out_specs=row_spec,
         ),
-        compiler_params=pltpu.CompilerParams(vmem_limit_bytes=48 << 20),
+        compiler_params=pltpu.CompilerParams(vmem_limit_bytes=24 << 20),
         name="mix",
     )(lengths, points, attended, o_weight, gain, up_weight, down_weight)
 
@@ -279,7 +280,7 @@
     rows, width = points.shape
     block_rows = rows // pattern.shape[0]
     gain1, gain2 = ln1_gain[None, :], ln2_gain[None, :]
-    to_right, to_left = pack(points, send_blocks[0], lengths, block_rows)
+    to_left, to_right = pack(points, send_blocks[0], lengths, block_rows)
     left = passed_along(to_right, "patch", 1)
     right = passed_along(to_left, "patch", -1)
     scale = LOG2E / math.sqrt(width // H)

time: 58.6 us -> 50.1 us (0.85)
  Pallas kernels: 45 us -> 37.8 us
  local copies, waits for them, and re-layouts: 3.78 us -> 0.12 us
  waiting for transfers between devices: 3.03 us -> 5.55 us
    unnamed x21 -> x19, local copies, waits for them, and re-layouts: 3.78 us -> 0.12 us
    pallas_call x1, Pallas kernels: 5.63 us -> 3.09 us  [project(): pl.pallas_call(functools.partial(project_kernel, scale), out_shape=(shape...]
    ppermute x2, waiting for transfers between devices: 3.03 us -> 5.55 us  [passed_along(): return lax.ppermute(array, axis, pairs)]
    pallas_call x1, Pallas kernels: 26.2 us -> 23.9 us  [attend(): pl.pallas_call(functools.partial(attend_kernel, block_rows, width // H),...]
    pallas_call x1, Pallas kernels: 9.47 us -> 7.86 us  [mix(): pl.pallas_call(mix_kernel, out_shape=jax.ShapeDtypeStruct((rows, width),...]
    pallas_call x1, Pallas kernels: 3.63 us -> 2.98 us  [pack(): pl.pallas_call(pack_kernel, out_shape=(shape, shape), grid_spec=pltpu.Pre...]
  transfers between devices with their start and end apart: 2 -> 2, of which waited for: 1 -> 1; matrix products, arithmetic and copies ran while one was open for 0% -> 0% of each run, Pallas kernels for 10% -> 6%
where the time goes in v2:
time: 50.1 us; the launch traced here: 49.9 us
  Pallas kernels  37.8 us (75%)
  starting transfers between devices  5.62 us (11%)
  waiting for transfers between devices  5.55 us (11%)
  between operations  0.78 us (2%)
    pallas_call x1, Pallas kernels, attend(): pl.pallas_call(functools.partial(attend_kernel, block_rows, width // H),...  23.9 us
    pallas_call x1, Pallas kernels, mix(): pl.pallas_call(mix_kernel, out_shape=jax.ShapeDtypeStruct((rows, width),...  7.86 us
    ppermute x2, starting transfers between devices, passed_along(): return lax.ppermute(array, axis, pairs)  5.62 us
    ppermute x2, waiting for transfers between devices, passed_along(): return lax.ppermute(array, axis, pairs)  5.55 us
    pallas_call x1, Pallas kernels, project(): pl.pallas_call(functools.partial(project_kernel, scale), out_shape=(shape...  3.09 us
    pallas_call x1, Pallas kernels, pack(): pl.pallas_call(pack_kernel, out_shape=(shape, shape), grid_spec=pltpu.Pre...  2.98 us
  transfers between devices with their start and end apart: 2, of which 1 were waited for; matrix products, arithmetic and copies ran while one was open for 0% of the time, Pallas kernels for 6%

profile of v2, /device:TPU:25, one launch (start us, length us, event | category | flops | bytes accessed | tf_op | source)
XLA Modules:
  0.0 49.9 jit_solution(10292463306098395479)
XLA Ops:
  0.7 0.0 copy-start.8
  0.7 0.0 copy-start
  0.7 0.0 copy-start.3
  0.7 0.0 copy-start.5
  0.7 0.0 copy-start.6
  0.7 3.0 %pack.1 = (bf16[384,512]{1,0:T(8,128)(2,1)}, bf16[384,512]{1,0:T(8,128)(2,1)}) custom-call(s32[2,3]{1,0:T(2,128)} %bitcast.6, s32[1]{0:T(128)S(6)} %copy.13.length_ref, bf16[1024,512]{1,0:T(8,128)(2,1)} %x_ref.3, bf16[1024,512]{1,0:T(8,128)(2,1)} %x_ref.3, bf16[1024,512]{1,0:T(8,128)(2,1)} %x_ref.3, bf16[1024,512]{1,0:T(8,128)(2,1)} %x_ref.3, ...), custom_call_target="tpu_custom_call" | custom-call | tf_op jit(solution)/shard_map/pack/pallas_call | solution.py:53
  3.7 3.7 %collective-permute-start = (bf16[384,512]{1,0:T(8,128)(2,1)}, bf16[384,512]{1,0:T(8,128)(2,1)S(1)}, u32[]{:S(2)}, u32[]{:S(2)}) collective-permute-start(bf16[384,512]{1,0:T(8,128)(2,1)} %get-tuple-element.13), channel_id=1, source_target_pairs={{0,1},{1,2},{2,3},{3,4},{4,5},{5,6},{6,7},{7,8},{8,9},{9,10},{10,1... | collective-permute-start | bytes 1179656 | tf_op jit(solution)/shard_map/ppermute | solution.py:22
  7.4 1.9 %collective-permute-start.1 = (bf16[384,512]{1,0:T(8,128)(2,1)}, bf16[384,512]{1,0:T(8,128)(2,1)S(1)}, u32[]{:S(2)}, u32[]{:S(2)}) collective-permute-start(bf16[384,512]{1,0:T(8,128)(2,1)} %get-tuple-element.14), channel_id=1, source_target_pairs={{1,0},{2,1},{3,2},{4,3},{5,4},{6,5},{7,6},{8,7},{9,8},{10,9},{11,1... | collective-permute-start | bytes 1179656 | tf_op jit(solution)/shard_map/ppermute | solution.py:22
  9.3 0.0 copy-done.8
  9.3 0.1 copy.12.pattern_ref
  9.4 0.0 copy-done
  9.4 0.0 copy-done.3
  9.4 0.0 copy-done.5
  9.4 0.0 copy-done.6
  9.4 3.1 %project.1 = (bf16[1024,512]{1,0:T(8,128)(2,1)S(1)}, bf16[1024,512]{1,0:T(8,128)(2,1)S(1)}, bf16[1024,512]{1,0:T(8,128)(2,1)S(1)}) custom-call(bf16[1024,512]{1,0:T(8,128)(2,1)S(1)} %copy-done, f32[1,512]{1,0:T(1,128)S(1)} %bitcast.3, bf16[2,512,512]{2,1,0:T(8,128)(2,1)S(1)} %copy-done.3, bf16[512,512]{1,0:T(8,128)(2,1)S(1)} %copy-done.5), custom_call_target="tpu_custom_call" | custom-call | flops 1610612736 | bytes 5767168 | tf_op jit(solution)/shard_map/project/pallas_call | solution.py:78
  12.5 0.0 collective-permute-done.left_ref
  12.5 5.5 %collective-permute-done.1.right_ref = bf16[384,512]{1,0:T(8,128)(2,1)S(1)} collective-permute-done((bf16[384,512]{1,0:T(8,128)(2,1)}, bf16[384,512]{1,0:T(8,128)(2,1)S(1)}, u32[]{:S(2)}, u32[]{:S(2)}) %collective-permute-start.1) | collective-permute-done | bytes 393248 | tf_op jit(solution)/shard_map/ppermute | solution.py:22
  18.1 0.0 copy-start.1
  18.1 0.0 copy-start.2
  18.1 0.0 copy-start.4
  18.1 0.0 copy-start.7
  18.1 23.9 %attend.1.a_ref = bf16[1024,512]{1,0:T(8,128)(2,1)S(1)} custom-call(s32[8,3]{1,0:T(8,128)S(1)} %copy.12.pattern_ref, s32[1]{0:T(128)S(6)} %copy.13.length_ref, bf16[1024,512]{1,0:T(8,128)(2,1)S(1)} %get-tuple-element.10.q_ref, bf16[1024,512]{1,0:T(8,128)(2,1)S(1)} %get-tuple-element.11.k_ref, bf16[1024,512]{1,0:T(8,128)(2,1)S(1)} %get-tuple-element.12.v_ref, ...), custom_call_target="tpu_custom_call" | custom-call | tf_op jit(solution)/shard_map/attend/pallas_call | solution.py:201
  42.0 0.0 copy-done.1
  42.0 0.0 copy-done.2
  42.0 0.0 copy-done.4
  42.0 0.0 copy-done.7
  42.0 7.9 %mix.1 = bf16[1024,512]{1,0:T(8,128)(2,1)} custom-call(s32[1]{0:T(128)S(6)} %copy.13.length_ref, bf16[1024,512]{1,0:T(8,128)(2,1)S(1)} %copy-done, bf16[1024,512]{1,0:T(8,128)(2,1)S(1)} %attend.1.a_ref, bf16[512,512]{1,0:T(8,128)(2,1)S(1)} %copy-done.4, f32[1,512]{1,0:T(1,128)S(1)} %bitcast.5, bf16[512,2048]{1,0:T(8,128)(2,1)S(1)} %copy-done.1, ...), custom_call_target="tpu_custom_call" | custom-call | tf_op jit(solution)/shard_map/mix/pallas_call | solution.py:246
Async XLA Ops:
  0.7 8.7 %copy-start.8 = (s32[8,3]{0,1:T(4,128)S(1)}, s32[8,3]{0,1:T(4,128)}, u32[]{:S(2)}) copy-start(s32[8,3]{0,1:T(4,128)} %param.14) | copy-start | bytes 292
  0.7 8.7 %copy-start = (bf16[1024,512]{1,0:T(8,128)(2,1)S(1)}, bf16[1024,512]{1,0:T(8,128)(2,1)}, u32[]{:S(2)}) copy-start(bf16[1024,512]{1,0:T(8,128)(2,1)} %x_ref.3) | copy-start | bytes 3145732
  0.7 8.7 %copy-start.3 = (bf16[2,512,512]{2,1,0:T(8,128)(2,1)S(1)}, bf16[2,512,512]{2,1,0:T(8,128)(2,1)}, u32[]{:S(2)}) copy-start(bf16[2,512,512]{2,1,0:T(8,128)(2,1)} %wk_ref.1) | copy-start | bytes 3145732
  0.7 8.7 %copy-start.5 = (bf16[512,512]{1,0:T(8,128)(2,1)S(1)}, bf16[512,512]{1,0:T(8,128)(2,1)}, u32[]{:S(2)}) copy-start(bf16[512,512]{1,0:T(8,128)(2,1)} %wv_ref.1) | copy-start | bytes 1572868
  0.7 8.7 %copy-start.6 = (f32[512]{0:T(512)S(1)}, f32[512]{0:T(512)}, u32[]{:S(2)}) copy-start(f32[512]{0:T(512)} %param.15) | copy-start | bytes 6148
  3.7 8.8 %collective-permute-start = (bf16[384,512]{1,0:T(8,128)(2,1)}, bf16[384,512]{1,0:T(8,128)(2,1)S(1)}, u32[]{:S(2)}, u32[]{:S(2)}) collective-permute-start(bf16[384,512]{1,0:T(8,128)(2,1)} %get-tuple-element.13), channel_id=1, source_target_pairs={{0,1},{1,2},{2,3},{3,4},{4,5},{5,6},{6,7},{7,8},{8,9},{9,10},{10,1... | collective-permute-start | bytes 1179656 | tf_op jit(solution)/shard_map/ppermute | solution.py:22
  7.4 10.7 %collective-permute-start.1 = (bf16[384,512]{1,0:T(8,128)(2,1)}, bf16[384,512]{1,0:T(8,128)(2,1)S(1)}, u32[]{:S(2)}, u32[]{:S(2)}) collective-permute-start(bf16[384,512]{1,0:T(8,128)(2,1)} %get-tuple-element.14), channel_id=1, source_target_pairs={{1,0},{2,1},{3,2},{4,3},{5,4},{6,5},{7,6},{8,7},{9,8},{10,9},{11,1... | collective-permute-start | bytes 1179656 | tf_op jit(solution)/shard_map/ppermute | solution.py:22
  18.1 23.9 %copy-start.1 = (bf16[512,2048]{1,0:T(8,128)(2,1)S(1)}, bf16[512,2048]{1,0:T(8,128)(2,1)}, u32[]{:S(2)}) copy-start(bf16[512,2048]{1,0:T(8,128)(2,1)} %up_ref.1) | copy-start | bytes 6291460
  18.1 23.9 %copy-start.2 = (bf16[2048,512]{1,0:T(8,128)(2,1)S(1)}, bf16[2048,512]{1,0:T(8,128)(2,1)}, u32[]{:S(2)}) copy-start(bf16[2048,512]{1,0:T(8,128)(2,1)} %down_ref.1) | copy-start | bytes 6291460
  18.1 23.9 %copy-start.4 = (bf16[512,512]{1,0:T(8,128)(2,1)S(1)}, bf16[512,512]{1,0:T(8,128)(2,1)}, u32[]{:S(2)}) copy-start(bf16[512,512]{1,0:T(8,128)(2,1)} %wo_ref.1) | copy-start | bytes 1572868
  18.1 23.9 %copy-start.7 = (f32[512]{0:T(512)S(1)}, f32[512]{0:T(512)}, u32[]{:S(2)}) copy-start(f32[512]{0:T(512)} %param.19) | copy-start | bytes 6148

commit v3 on v2

--- a/solution.py
+++ b/solution.py
@@ -71,7 +71,7 @@
     v_out[...] = jnp.dot(normed, v_ref[...], preferred_element_type=jnp.float32).astype(v_out.dtype)
 
 
-def project(points, gain, qk_weight, v_weight, scale, tile=256):
+def project(points, gain, qk_weight, v_weight, scale, tile=512):
     rows, width = points.shape
     shape = jax.ShapeDtypeStruct((rows, width), jnp.bfloat16)
     row_spec = pl.BlockSpec((tile, width), lambda i: (i, 0))
@@ -239,7 +239,7 @@
     out_ref[...] = jnp.where(position < length_ref[0], result, 0.0).astype(out_ref.dtype)
 
 
-def mix(points, attended, lengths, o_weight, gain, up_weight, down_weight, tile=256):
+def mix(points, attended, lengths, o_weight, gain, up_weight, down_weight, tile=512):
     rows, width = points.shape
     row_spec = pl.BlockSpec((tile, width), lambda i, *_: (i, 0))
     whole = lambda shape: pl.BlockSpec(shape, lambda i, *_: (0,) * len(shape))

time: 50.1 us -> 49 us (0.978)
  Pallas kernels: 37.8 us -> 36.2 us
  waiting for transfers between devices: 5.55 us -> 6.12 us
    pallas_call x1, Pallas kernels: 7.86 us -> 6.8 us  [mix(): pl.pallas_call(mix_kernel, out_shape=jax.ShapeDtypeStruct((rows, width),...]
    ppermute x2, waiting for transfers between devices: 5.55 us -> 6.12 us  [passed_along(): return lax.ppermute(array, axis, pairs)]
    pallas_call x1, Pallas kernels: 3.09 us -> 2.52 us  [project(): pl.pallas_call(functools.partial(project_kernel, scale), out_shape=(shape...]
  transfers between devices with their start and end apart: 2 -> 2, of which waited for: 1 -> 2; matrix products, arithmetic and copies ran while one was open for 0% -> 0% of each run, Pallas kernels for 6% -> 5%
where the time goes in v3:
time: 49 us; the launch traced here: 48.8 us
  Pallas kernels  36.2 us (74%)
  waiting for transfers between devices  6.12 us (12%)
  starting transfers between devices  5.62 us (11%)
  between operations  0.78 us (2%)
    pallas_call x1, Pallas kernels, attend(): pl.pallas_call(functools.partial(attend_kernel, block_rows, width // H),...  23.9 us
    pallas_call x1, Pallas kernels, mix(): pl.pallas_call(mix_kernel, out_shape=jax.ShapeDtypeStruct((rows, width),...  6.8 us
    ppermute x2, waiting for transfers between devices, passed_along(): return lax.ppermute(array, axis, pairs)  6.12 us
    ppermute x2, starting transfers between devices, passed_along(): return lax.ppermute(array, axis, pairs)  5.62 us
    pallas_call x1, Pallas kernels, pack(): pl.pallas_call(pack_kernel, out_shape=(shape, shape), grid_spec=pltpu.Pre...  2.98 us
    pallas_call x1, Pallas kernels, project(): pl.pallas_call(functools.partial(project_kernel, scale), out_shape=(shape...  2.52 us
  transfers between devices with their start and end apart: 2, of which 2 were waited for; matrix products, arithmetic and copies ran while one was open for 0% of the time, Pallas kernels for 5%

profile of v3, /device:TPU:25, one launch (start us, length us, event | category | flops | bytes accessed | tf_op | source)
XLA Modules:
  0.0 48.8 jit_solution(130326917105200582)
XLA Ops:
  0.7 0.0 copy-start.8
  0.7 0.0 copy-start
  0.7 0.0 copy-start.3
  0.7 0.0 copy-start.5
  0.7 0.0 copy-start.6
  0.7 3.0 %pack.1 = (bf16[384,512]{1,0:T(8,128)(2,1)}, bf16[384,512]{1,0:T(8,128)(2,1)}) custom-call(s32[2,3]{1,0:T(2,128)} %bitcast.6, s32[1]{0:T(128)S(6)} %copy.13.length_ref, bf16[1024,512]{1,0:T(8,128)(2,1)} %x_ref.3, bf16[1024,512]{1,0:T(8,128)(2,1)} %x_ref.3, bf16[1024,512]{1,0:T(8,128)(2,1)} %x_ref.3, bf16[1024,512]{1,0:T(8,128)(2,1)} %x_ref.3, ...), custom_call_target="tpu_custom_call" | custom-call | tf_op jit(solution)/shard_map/pack/pallas_call | solution.py:53
  3.7 3.7 %collective-permute-start = (bf16[384,512]{1,0:T(8,128)(2,1)}, bf16[384,512]{1,0:T(8,128)(2,1)S(1)}, u32[]{:S(2)}, u32[]{:S(2)}) collective-permute-start(bf16[384,512]{1,0:T(8,128)(2,1)} %get-tuple-element.13), channel_id=1, source_target_pairs={{0,1},{1,2},{2,3},{3,4},{4,5},{5,6},{6,7},{7,8},{8,9},{9,10},{10,1... | collective-permute-start | bytes 1179656 | tf_op jit(solution)/shard_map/ppermute | solution.py:22
  7.4 1.9 %collective-permute-start.1 = (bf16[384,512]{1,0:T(8,128)(2,1)}, bf16[384,512]{1,0:T(8,128)(2,1)S(1)}, u32[]{:S(2)}, u32[]{:S(2)}) collective-permute-start(bf16[384,512]{1,0:T(8,128)(2,1)} %get-tuple-element.14), channel_id=1, source_target_pairs={{1,0},{2,1},{3,2},{4,3},{5,4},{6,5},{7,6},{8,7},{9,8},{10,9},{11,1... | collective-permute-start | bytes 1179656 | tf_op jit(solution)/shard_map/ppermute | solution.py:22
  9.3 0.0 copy-done.8
  9.3 0.1 copy.12.pattern_ref
  9.4 0.0 copy-done
  9.4 0.0 copy-done.3
  9.4 0.0 copy-done.5
  9.4 0.0 copy-done.6
  9.4 2.5 %project.1 = (bf16[1024,512]{1,0:T(8,128)(2,1)S(1)}, bf16[1024,512]{1,0:T(8,128)(2,1)S(1)}, bf16[1024,512]{1,0:T(8,128)(2,1)S(1)}) custom-call(bf16[1024,512]{1,0:T(8,128)(2,1)S(1)} %copy-done, f32[1,512]{1,0:T(1,128)S(1)} %bitcast.3, bf16[2,512,512]{2,1,0:T(8,128)(2,1)S(1)} %copy-done.3, bf16[512,512]{1,0:T(8,128)(2,1)S(1)} %copy-done.5), custom_call_target="tpu_custom_call" | custom-call | flops 1610612736 | bytes 5767168 | tf_op jit(solution)/shard_map/project/pallas_call | solution.py:78
  12.0 0.4 collective-permute-done.left_ref
  12.4 5.7 %collective-permute-done.1.right_ref = bf16[384,512]{1,0:T(8,128)(2,1)S(1)} collective-permute-done((bf16[384,512]{1,0:T(8,128)(2,1)}, bf16[384,512]{1,0:T(8,128)(2,1)S(1)}, u32[]{:S(2)}, u32[]{:S(2)}) %collective-permute-start.1) | collective-permute-done | bytes 393248 | tf_op jit(solution)/shard_map/ppermute | solution.py:22
  18.1 0.0 copy-start.1
  18.1 0.0 copy-start.2
  18.1 0.0 copy-start.4
  18.1 0.0 copy-start.7
  18.1 23.9 %attend.1.a_ref = bf16[1024,512]{1,0:T(8,128)(2,1)S(1)} custom-call(s32[8,3]{1,0:T(8,128)S(1)} %copy.12.pattern_ref, s32[1]{0:T(128)S(6)} %copy.13.length_ref, bf16[1024,512]{1,0:T(8,128)(2,1)S(1)} %get-tuple-element.10.q_ref, bf16[1024,512]{1,0:T(8,128)(2,1)S(1)} %get-tuple-element.11.k_ref, bf16[1024,512]{1,0:T(8,128)(2,1)S(1)} %get-tuple-element.12.v_ref, ...), custom_call_target="tpu_custom_call" | custom-call | tf_op jit(solution)/shard_map/attend/pallas_call | solution.py:201
  42.0 0.0 copy-done.1
  42.0 0.0 copy-done.2
  42.0 0.0 copy-done.4
  42.0 0.0 copy-done.7
  42.0 6.8 %mix.1 = bf16[1024,512]{1,0:T(8,128)(2,1)} custom-call(s32[1]{0:T(128)S(6)} %copy.13.length_ref, bf16[1024,512]{1,0:T(8,128)(2,1)S(1)} %copy-done, bf16[1024,512]{1,0:T(8,128)(2,1)S(1)} %attend.1.a_ref, bf16[512,512]{1,0:T(8,128)(2,1)S(1)} %copy-done.4, f32[1,512]{1,0:T(1,128)S(1)} %bitcast.5, bf16[512,2048]{1,0:T(8,128)(2,1)S(1)} %copy-done.1, ...), custom_call_target="tpu_custom_call" | custom-call | tf_op jit(solution)/shard_map/mix/pallas_call | solution.py:246
Async XLA Ops:
  0.7 8.7 %copy-start.8 = (s32[8,3]{0,1:T(4,128)S(1)}, s32[8,3]{0,1:T(4,128)}, u32[]{:S(2)}) copy-start(s32[8,3]{0,1:T(4,128)} %param.14) | copy-start | bytes 292
  0.7 8.7 %copy-start = (bf16[1024,512]{1,0:T(8,128)(2,1)S(1)}, bf16[1024,512]{1,0:T(8,128)(2,1)}, u32[]{:S(2)}) copy-start(bf16[1024,512]{1,0:T(8,128)(2,1)} %x_ref.3) | copy-start | bytes 3145732
  0.7 8.7 %copy-start.3 = (bf16[2,512,512]{2,1,0:T(8,128)(2,1)S(1)}, bf16[2,512,512]{2,1,0:T(8,128)(2,1)}, u32[]{:S(2)}) copy-start(bf16[2,512,512]{2,1,0:T(8,128)(2,1)} %wk_ref.1) | copy-start | bytes 3145732
  0.7 8.7 %copy-start.5 = (bf16[512,512]{1,0:T(8,128)(2,1)S(1)}, bf16[512,512]{1,0:T(8,128)(2,1)}, u32[]{:S(2)}) copy-start(bf16[512,512]{1,0:T(8,128)(2,1)} %wv_ref.1) | copy-start | bytes 1572868
  0.7 8.7 %copy-start.6 = (f32[512]{0:T(512)S(1)}, f32[512]{0:T(512)}, u32[]{:S(2)}) copy-start(f32[512]{0:T(512)} %param.15) | copy-start | bytes 6148
  3.7 8.7 %collective-permute-start = (bf16[384,512]{1,0:T(8,128)(2,1)}, bf16[384,512]{1,0:T(8,128)(2,1)S(1)}, u32[]{:S(2)}, u32[]{:S(2)}) collective-permute-start(bf16[384,512]{1,0:T(8,128)(2,1)} %get-tuple-element.13), channel_id=1, source_target_pairs={{0,1},{1,2},{2,3},{3,4},{4,5},{5,6},{6,7},{7,8},{8,9},{9,10},{10,1... | collective-permute-start | bytes 1179656 | tf_op jit(solution)/shard_map/ppermute | solution.py:22
  7.4 10.7 %collective-permute-start.1 = (bf16[384,512]{1,0:T(8,128)(2,1)}, bf16[384,512]{1,0:T(8,128)(2,1)S(1)}, u32[]{:S(2)}, u32[]{:S(2)}) collective-permute-start(bf16[384,512]{1,0:T(8,128)(2,1)} %get-tuple-element.14), channel_id=1, source_target_pairs={{1,0},{2,1},{3,2},{4,3},{5,4},{6,5},{7,6},{8,7},{9,8},{10,9},{11,1... | collective-permute-start | bytes 1179656 | tf_op jit(solution)/shard_map/ppermute | solution.py:22
  18.1 23.9 %copy-start.1 = (bf16[512,2048]{1,0:T(8,128)(2,1)S(1)}, bf16[512,2048]{1,0:T(8,128)(2,1)}, u32[]{:S(2)}) copy-start(bf16[512,2048]{1,0:T(8,128)(2,1)} %up_ref.1) | copy-start | bytes 6291460
  18.1 23.9 %copy-start.2 = (bf16[2048,512]{1,0:T(8,128)(2,1)S(1)}, bf16[2048,512]{1,0:T(8,128)(2,1)}, u32[]{:S(2)}) copy-start(bf16[2048,512]{1,0:T(8,128)(2,1)} %down_ref.1) | copy-start | bytes 6291460
  18.1 23.9 %copy-start.4 = (bf16[512,512]{1,0:T(8,128)(2,1)S(1)}, bf16[512,512]{1,0:T(8,128)(2,1)}, u32[]{:S(2)}) copy-start(bf16[512,512]{1,0:T(8,128)(2,1)} %wo_ref.1) | copy-start | bytes 1572868
  18.1 23.9 %copy-start.7 = (f32[512]{0:T(512)S(1)}, f32[512]{0:T(512)}, u32[]{:S(2)}) copy-start(f32[512]{0:T(512)} %param.19) | copy-start | bytes 6148
